TPU v7x, 32 devices: a whole 2x2x4 slice. The times are simulated.
32 devices in a mesh: mem: 4 (over x, core), lon: 8 (over z, y).
Axes of the slice: x: 2, y: 2, z: 4, core: 2. Of those that a mesh axis runs over, the one named last changes fastest.
Arguments:
- controls: bfloat16 [2048, 32, 1024], P('lon', 'mem'), may hold values from -6 to 6
- perturbations: bfloat16 [2048, 32, 1024], P(None, 'mem', 'lon'), may hold values from -0.59765625 to 0.59765625
- lat_factor: bfloat16 [1024, 1024], P('mem'), may hold values from -0.09375 to 0.09375
- lon_factor: bfloat16 [2048, 2048], P('mem'), may hold values from -0.0625 to 0.0625
- obs_index: int32 [4, 8, 32768], P('mem', 'lon'), may hold values from 0 to 65535
- obs_weight: float32 [4, 8, 32768], P('mem', 'lon'), may hold values from 1 to 30
- obs_count: int32 [4, 8], P('mem', 'lon'), may hold values from 8193 to 32768, as said below
Outputs:
- hessian_product: float32 [2048, 32, 1024], P('lon', 'mem')
Inputs may be any that keep to these rules, and one draw needn't show every extreme that they name: `obs_index`: several slots may name one grid point; grid points are numbered with latitude fastest within a tile of 512 by 128. `obs_count`: slots 0 to count - 1 of a tile are in use; some tile uses all 32768 slots.
All inputs are finite; a program needn't handle non-finite values.
Results may differ from a plain program's by a relative error of at most 0.008.
Values may be sent and summed in bfloat16 or wider, within the bound.
No kernel may reach another device: no remote copies, remote signals or barrier semaphores. Data moves between devices by JAX's collectives and lax.ppermute only.
A program may use at most 128 MiB of HBM per device.

v0:
```python
import jax
import jax.numpy as jnp
from jax import lax
from jax.sharding import PartitionSpec as P


def observe(grid_field, index_rows, weight_rows, count_rows):
    tile_count, slot_count = index_rows.shape
    flattened = grid_field.reshape(-1)
    tile_cells = flattened.shape[0] // tile_count
    where_at = index_rows + (jnp.arange(tile_count, dtype=jnp.int32) * tile_cells)[:, None]
    in_use = jnp.arange(slot_count, dtype=jnp.int32)[None, :] < count_rows[:, None]
    picked = flattened[where_at]
    values = jnp.where(in_use, weight_rows * picked, jnp.zeros_like(picked))
    return (
        jnp.zeros_like(flattened)
        .at[where_at.reshape(-1)]
        .add(values.reshape(-1))
        .reshape(grid_field.shape)
    )


def local(controls, perturbations, lat_factor, lon_factor, obs_index, obs_weight, obs_count):
    lon_dev, mem_dev, lat_all = controls.shape
    lat_full = lax.all_gather(lat_factor, "mem", axis=0, tiled=True)
    control_rows = controls.reshape(lon_dev * mem_dev, lat_all)
    banded = (
        control_rows.astype(jnp.float32)
        + lax.dot_general(
            control_rows, lat_full, (((1,), (1,)), ((), ())), preferred_element_type=jnp.float32
        )
    ).astype(jnp.bfloat16)
    moved = lax.all_to_all(
        banded.reshape(lon_dev, mem_dev, lat_all), "lon", split_axis=2, concat_axis=0, tiled=True
    )
    lon_all, _, lat_band = moved.shape
    columns = moved.reshape(lon_all, mem_dev * lat_band)
    lon_full = lax.all_gather(lon_factor, "mem", axis=0, tiled=True)
    spread_fwd = jnp.dot(lon_full, columns, preferred_element_type=jnp.float32)
    localized = columns.astype(jnp.float32) + spread_fwd
    weighted_fwd = (
        perturbations.reshape(lon_all, mem_dev * lat_band).astype(jnp.float32) * localized
    )
    partial_sum = jnp.sum(weighted_fwd.reshape(lon_all, mem_dev, lat_band), axis=1)
    slot_count = obs_index.shape[-1]
    tile_sum = lax.psum_scatter(partial_sum, "mem", scatter_dimension=0, tiled=True)
    grad_tile = observe(
        tile_sum,
        obs_index.reshape(-1, slot_count),
        obs_weight.reshape(-1, slot_count),
        obs_count.reshape(-1),
    ).astype(jnp.bfloat16)
    gradient = lax.all_gather(grad_tile, "mem", axis=0, tiled=True)
    weighted = (
        (perturbations.astype(jnp.float32) * gradient.astype(jnp.float32)[:, None, :])
        .astype(jnp.bfloat16)
        .reshape(lon_all, mem_dev * lat_band)
    )
    spread_back = lax.dot_general(
        lon_full, weighted, (((0,), (0,)), ((), ())), preferred_element_type=jnp.float32
    )
    spread = (
        (weighted.astype(jnp.float32) + spread_back)
        .astype(jnp.bfloat16)
        .reshape(lon_all, mem_dev, lat_band)
    )
    returned = lax.all_to_all(spread, "lon", split_axis=0, concat_axis=2, tiled=True)
    back_rows = returned.reshape(lon_dev * mem_dev, lat_all)
    result = (
        control_rows.astype(jnp.float32)
        + back_rows.astype(jnp.float32)
        + jnp.dot(back_rows, lat_full, preferred_element_type=jnp.float32)
    )
    return result.reshape(lon_dev, mem_dev, lat_all)


def solution(mesh):
    in_specs = (
        P("lon", "mem", None),
        P(None, "mem", "lon"),
        P("mem", None),
        P("mem", None),
        P("mem", "lon", None),
        P("mem", "lon", None),
        P("mem", "lon"),
    )
    out_specs = P("lon", "mem", None)
    return jax.shard_map(local, mesh=mesh, in_specs=in_specs, out_specs=out_specs, check_vma=False)
```

profile of v0, /device:TPU:0, one launch (start us, length us, event | category | flops | bytes accessed | tf_op | source)
XLA Modules:
  0.0 709.8 jit_solution(16194023989570546402)
XLA Ops:
  6.5 0.7 all-gather.3.cloned.1.call-update
  7.3 0.7 all-gather.5.cloned.1.call-update
  8.0 26.2 %all-gather.3.cloned.1.call-done = bf16[1024,1024]{1,0:T(8,128)(2,1)} async-done(((bf16[256,1024]{1,0:T(8,128)(2,1)}), bf16[1024,1024]{1,0:T(8,128)(2,1)}) %all-gather.3.cloned.1.call-update) | async-done | bytes 2097168 | tf_op jit(solution)/shard_map/all_gather | solution.py:25
  34.2 10.8 %fusion.5 = bf16[256,8,1024]{2,1,0:T(8,128)(2,1)} fusion(bf16[256,8,1024]{2,1,0:T(8,128)(2,1)} %param.7, bf16[1024,1024]{1,0:T(8,128)(2,1)} %all-gather.3.cloned.1.call-done), kind=kOutput, calls=%fused_computation.12 | convolution fusion | flops 4301258752 | bytes 10485760 | tf_op jit(solution)/shard_map/dot_general | solution.py:29
  45.0 7.5 %copy.30 = bf16[256,8,1024]{0,1,2:T(8,128)(2,1)} copy(bf16[256,8,1024]{2,1,0:T(8,128)(2,1)} %fusion.5) | data formatting | bytes 8388608 | tf_op jit(solution)/shard_map/reshape | solution.py:34
  52.4 5.6 all-to-all-start
  58.0 0.2 reduce-scatter.2.cloned.1.call-start
  58.2 7.7 %copy.29 = f32[2048,8,128]{0,2,1:T(8,128)} copy(bf16[2048,8,128]{2,1,0:T(8,128)(2,1)} %param.8) | data formatting | bytes 12582912 | tf_op jit(solution)/shard_map/convert_element_type | solution.py:55
  66.1 85.6 %all-to-all-done = bf16[256,8,1024]{0,1,2:T(8,128)(2,1)} async-done(((bf16[256,8,1024]{0,1,2:T(8,128)(2,1)}), bf16[256,8,1024]{0,1,2:T(8,128)(2,1)}, u32[]{:S(2)}, u32[]{:S(2)}) %all-to-all-start) | async-done | bytes 4194336 | tf_op jit(solution)/shard_map/all_to_all | solution.py:33
  151.7 4.6 copy.31
  156.2 3.4 copy.36
  159.6 17.6 %fusion.4 = f32[2048,1024]{0,1:T(8,128)} fusion(f32[2048,8,128]{0,2,1:T(8,128)} %copy.29, bf16[2048,1024]{0,1:T(8,128)(2,1)} %bitcast.61, bf16[2048,2048]{1,0:T(8,128)(2,1)} %all-gather.5.cloned.1.call-done), kind=kOutput, calls=%fused_computation.10 | convolution fusion | flops 8596226048 | bytes 29360128 | tf_op jit(solution)/shard_map/dot_general | solution.py:39
  177.2 5.1 reduce_sum.9
  183.2 22.4 %reduce-scatter.2.cloned.1.call-done = f32[512,128]{0,1:T(8,128)} async-done(((f32[2048,128]{0,1:T(8,128)}), f32[512,128]{0,1:T(8,128)}) %reduce-scatter.2.cloned.1.call-update) | async-done | bytes 262160 | tf_op jit(solution)/shard_map/reduce_scatter | solution.py:46
  205.6 1.1 copy.32
  206.7 180.5 %gather_fusion = f32[32768]{0:T(1024)S(1)} fusion(f32[65536]{0:T(1024)S(1)} %bitcast.58, s32[32768]{0:T(1024)S(1)} %broadcast_clamp_fusion), kind=kCustom, calls=%fused_computation | custom fusion | bytes 393216 | tf_op jit(solution)/shard_map/gather | solution.py:13
  387.3 171.1 %scatter_custom_fusion = f32[65536]{0:T(1024)S(1)} fusion(s32[32768]{0:T(1024)S(1)} %bitcast.67, f32[32768]{0:T(1024)S(1)} %multiply_select_fusion, f32[]{:T(128)} %constant.3.clone.1), kind=kCustom, calls=%fused_computation.23 | custom fusion | flops 32768 | bytes 262148 | tf_op jit(solution)/shard_map/scatter-add | solution.py:18
  558.4 6.8 all_gather.11
  565.3 4.0 multiply_convert_fusion
  569.3 6.7 copy.33
  576.0 14.4 %fusion.3 = bf16[2048,1024]{0,1:T(8,128)(2,1)} fusion(bf16[2048,1024]{0,1:T(8,128)(2,1)} %bitcast.62, bf16[2048,2048]{1,0:T(8,128)(2,1)} %all-gather.5.cloned.1.call-done), kind=kOutput, calls=%fused_computation.8 | convolution fusion | flops 8596226048 | bytes 16777216 | tf_op jit(solution)/shard_map/dot_general | solution.py:59
  590.4 6.7 copy.34
  597.1 99.4 %all_to_all.30 = bf16[2048,8,128]{2,1,0:T(8,128)(2,1)S(1)} all-to-all(bf16[2048,8,128]{2,1,0:T(8,128)(2,1)} %copy.34), channel_id=1, replica_groups=mesh['mem'=4,'lon'=8] {'lon'}, dimensions={0} | all-to-all | bytes 8388608 | tf_op jit(solution)/shard_map/all_to_all | solution.py:67
  696.6 6.7 fusion.2
  (18 shorter events, 0.5 us)
Async XLA Ops:
  6.5 27.7 %all-gather.3.cloned.1.call-start = ((), (), s32[]{:S(2)}) async-start(), calls=%async_computation.3 | async-start | bytes 2621440 | tf_op jit(solution)/shard_map/all_gather | solution.py:25
  7.3 152.4 %all-gather.5.cloned.1.call-start = ((), (), s32[]{:S(2)}) async-start(), calls=%async_computation.4 | async-start | bytes 10485760 | tf_op jit(solution)/shard_map/all_gather | solution.py:38
  52.4 99.2 %all-to-all-start = ((bf16[256,8,1024]{0,1,2:T(8,128)(2,1)}), bf16[256,8,1024]{0,1,2:T(8,128)(2,1)}, u32[]{:S(2)}, u32[]{:S(2)}) async-start(bf16[256,8,1024]{0,1,2:T(8,128)(2,1)} %copy.30), calls=%async_computation | async-start | bytes 8388608 | tf_op jit(solution)/shard_map/all_to_all | solution.py:33
  58.0 7.9 %copy-start = (s32[1,1,32768]{2,1,0:T(1,128)S(1)}, s32[1,1,32768]{2,1,0:T(1,128)}, u32[]{:S(2)}) copy-start(s32[1,1,32768]{2,1,0:T(1,128)} %param.11) | copy-start | bytes 393220
  58.0 147.6 %reduce-scatter.2.cloned.1.call-start = ((), (), s32[]{:S(2)}) async-start(), calls=%async_computation.5 | async-start | bytes 1310720 | tf_op jit(solution)/shard_map/reduce_scatter | solution.py:46
  206.7 180.6 %copy-start.1 = (f32[1,1,32768]{2,1,0:T(1,128)S(1)}, f32[1,1,32768]{2,1,0:T(1,128)}, u32[]{:S(2)}) copy-start(f32[1,1,32768]{2,1,0:T(1,128)} %param.12) | copy-start | bytes 393220
  597.1 99.4 %copy-start.2 = (bf16[256,8,1024]{2,1,0:T(8,128)(2,1)S(1)}, bf16[256,8,1024]{2,1,0:T(8,128)(2,1)}, u32[]{:S(2)}) copy-start(bf16[256,8,1024]{2,1,0:T(8,128)(2,1)} %param.7) | copy-start | bytes 12582916
  597.1 99.4 %copy-start.3 = (bf16[1024,1024]{1,0:T(8,128)(2,1)S(1)}, bf16[1024,1024]{1,0:T(8,128)(2,1)}, u32[]{:S(2)}) copy-start(bf16[1024,1024]{1,0:T(8,128)(2,1)} %all-gather.3.cloned.1.call-done) | copy-start | bytes 6291460
Sparse Core Ops, SparseCore 0:
  8.9 25.2 all-gather.2
  35.8 58.2 all-gather.4
  182.5 23.0 reduce-scatter.1
where the time goes:
time: 711 us; the launch traced here: 710 us
  local copies, waits for them, and re-layouts  218 us (31%)
  other arithmetic  181 us (25%)
  waiting for transfers between devices  136 us (19%)
  blocking collectives  106 us (15%)
  matrix products  49.4 us (7%)
  between operations  13.8 us (2%)
    gather x1, local copies, waits for them, and re-layouts, observe(): picked = flattened[where_at]  181 us
    scatter-add x1, other arithmetic, observe(): return jnp.zeros_like(flattened).at[where_at.reshape(-1)].add(values.resh...  171 us
    all_to_all x1, blocking collectives, local(): lax.all_to_all(spread, 'lon', split_axis=0, concat_axis=2, tiled=True)  99.4 us
    all_to_all x1, waiting for transfers between devices, local(): lax.all_to_all(banded.reshape(lon_dev, mem_dev, lat_all), 'lon', split_ax...  85.6 us
    all_gather x1, waiting for transfers between devices, local(): lat_full = lax.all_gather(lat_factor, 'mem', axis=0, tiled=True)  26.2 us
    reduce_scatter x1, waiting for transfers between devices, local(): lax.psum_scatter(partial_sum, 'mem', scatter_dimension=0, tiled=True)  22.4 us
    dot_general x1, matrix products, local(): spread_fwd = jnp.dot(lon_full, columns, preferred_element_type=jnp.float32)  17.6 us
    dot_general x1, matrix products, local(): lax.dot_general(lon_full, weighted, (((0,), (0,)), ((), ())), preferred_e...  14.4 us
  transfers between devices with their start and end apart: 4, of which 3 were waited for; matrix products, arithmetic and copies ran while one was open for 5% of the time, Pallas kernels for 0%

commit v1 on v0

--- a/solution.py
+++ b/solution.py
@@ -30,9 +30,10 @@
             control_rows, lat_full, (((1,), (1,)), ((), ())), preferred_element_type=jnp.float32
         )
     ).astype(jnp.bfloat16)
-    moved = lax.all_to_all(
-        banded.reshape(lon_dev, mem_dev, lat_all), "lon", split_axis=2, concat_axis=0, tiled=True
-    )
+    x = banded.reshape(lon_dev, mem_dev, lat_all)
+    pieces = jnp.split(x, lax.axis_size("lon"), axis=2)
+    arrived = lax.all_to_all(jnp.stack(pieces), "lon", 0, 0)
+    moved = jnp.concatenate(arrived, axis=0)
     lon_all, _, lat_band = moved.shape
     columns = moved.reshape(lon_all, mem_dev * lat_band)
     lon_full = lax.all_gather(lon_factor, "mem", axis=0, tiled=True)

time: 711 us -> 712 us (level)
    unnamed x9 -> x16, local copies, waits for them, and re-layouts: 3.42 us -> 11.9 us
    reshape x1 -> x0, local copies, waits for them, and re-layouts: 7.47 us -> none  [local(): banded.reshape(lon_dev, mem_dev, lat_all)]
    another operation x0 -> x2, local copies, waits for them, and re-layouts: none -> 7.46 us  [the longest x1 6.51 us: local(): columns = moved.reshape(lon_all, mem_dev * lat_band)]
where the time goes in v1:
time: 712 us; the launch traced here: 711 us
  local copies, waits for them, and re-layouts  222 us (31%)
  other arithmetic  181 us (25%)
  waiting for transfers between devices  135 us (19%)
  blocking collectives  106 us (15%)
  matrix products  47.3 us (7%)
  between operations  13.9 us (2%)
    gather x1, local copies, waits for them, and re-layouts, observe(): picked = flattened[where_at]  181 us
    scatter-add x1, other arithmetic, observe(): return jnp.zeros_like(flattened).at[where_at.reshape(-1)].add(values.resh...  171 us
    all_to_all x1, blocking collectives, local(): lax.all_to_all(spread, 'lon', split_axis=0, concat_axis=2, tiled=True)  99.4 us
    all_to_all x1, waiting for transfers between devices, local(): arrived = lax.all_to_all(jnp.stack(pieces), 'lon', 0, 0)  85.6 us
    all_gather x1, waiting for transfers between devices, local(): lat_full = lax.all_gather(lat_factor, 'mem', axis=0, tiled=True)  26.2 us
    reduce_scatter x1, waiting for transfers between devices, local(): lax.psum_scatter(partial_sum, 'mem', scatter_dimension=0, tiled=True)  22.2 us
    dot_general x1, matrix products, local(): spread_fwd = jnp.dot(lon_full, columns, preferred_element_type=jnp.float32)  17.6 us
    dot_general x1, matrix products, local(): lax.dot_general(lon_full, weighted, (((0,), (0,)), ((), ())), preferred_e...  14.4 us
  transfers between devices with their start and end apart: 4, of which 3 were waited for; matrix products, arithmetic and copies ran while one was open for 5% of the time, Pallas kernels for 0%

profile of v1, /device:TPU:0, one launch (start us, length us, event | category | flops | bytes accessed | tf_op | source)
XLA Modules:
  0.0 711.4 jit_solution(10434496759606298323)
XLA Ops:
  8.0 26.2 %all-gather.3.cloned.1.call-done = bf16[1024,1024]{1,0:T(8,128)(2,1)} async-done(((bf16[256,1024]{1,0:T(8,128)(2,1)}), bf16[1024,1024]{1,0:T(8,128)(2,1)}) %all-gather.3.cloned.1.call-update) | async-done | bytes 2097168 | tf_op jit(solution)/shard_map/all_gather | solution.py:25
  34.2 8.6 %fusion.5 = bf16[256,8,1024]{2,1,0:T(8,128)(2,1)S(1)} fusion(bf16[256,8,1024]{2,1,0:T(8,128)(2,1)} %param.7, bf16[1024,1024]{1,0:T(8,128)(2,1)} %all-gather.3.cloned.1.call-done), kind=kOutput, calls=%fused_computation.12 | convolution fusion | flops 4301258752 | bytes 10485760 | tf_op jit(solution)/shard_map/dot_general | solution.py:29
  42.8 1.0 fusion.22
  43.8 1.0 fusion.21
  46.6 1.0 fusion.18
  49.4 0.9 fusion.15
  50.4 5.5 all-to-all-start
  56.1 7.7 %copy.21 = f32[2048,8,128]{0,2,1:T(8,128)} copy(bf16[2048,8,128]{2,1,0:T(8,128)(2,1)} %param.8) | data formatting | bytes 12582912 | tf_op jit(solution)/shard_map/convert_element_type | solution.py:56
  63.9 85.6 %all-to-all-done = bf16[8,256,8,128]{3,2,1,0:T(8,128)(2,1)} async-done(((bf16[8,256,8,128]{3,2,1,0:T(8,128)(2,1)}), bf16[8,256,8,128]{3,2,1,0:T(8,128)(2,1)}, u32[]{:S(2)}, u32[]{:S(2)}) %all-to-all-start) | async-done | bytes 4194336 | tf_op jit(solution)/shard_map/all_to_all | solution.py:35
  149.6 5.2 copy.38
  154.8 6.5 copy.27
  161.3 17.6 %fusion.4 = f32[2048,1024]{0,1:T(8,128)} fusion(f32[2048,8,128]{0,2,1:T(8,128)} %copy.21, bf16[2048,1024]{0,1:T(8,128)(2,1)} %copy.27, bf16[2048,2048]{1,0:T(8,128)(2,1)} %all-gather.5.cloned.1.call-done, bf16[256,8,8,128]{3,2,1,0:T(8,128)(2,1)} %bitcast.30), kind=kOutput, calls=%fused_computation.10 | convolution fusion | flops 8596226048 | bytes 33554432 | tf_op jit(solution)/shard_map/dot_general | solution.py:40
  179.0 5.1 reduce_sum.9
  185.0 22.2 %reduce-scatter.2.cloned.1.call-done = f32[512,128]{0,1:T(8,128)} async-done(((f32[2048,128]{0,1:T(8,128)}), f32[512,128]{0,1:T(8,128)}) %reduce-scatter.2.cloned.1.call-update) | async-done | bytes 262160 | tf_op jit(solution)/shard_map/reduce_scatter | solution.py:47
  207.2 1.1 copy.23
  208.3 180.5 %gather_fusion = f32[32768]{0:T(1024)S(1)} fusion(f32[65536]{0:T(1024)S(1)} %bitcast.88, s32[32768]{0:T(1024)S(1)} %broadcast_clamp_fusion), kind=kCustom, calls=%fused_computation | custom fusion | bytes 393216 | tf_op jit(solution)/shard_map/gather | solution.py:13
  388.9 171.1 %scatter_custom_fusion = f32[65536]{0:T(1024)S(1)} fusion(s32[32768]{0:T(1024)S(1)} %bitcast.96, f32[32768]{0:T(1024)S(1)} %multiply_select_fusion, f32[]{:T(128)} %constant.3.clone.1), kind=kCustom, calls=%fused_computation.40 | custom fusion | flops 32768 | bytes 262148 | tf_op jit(solution)/shard_map/scatter-add | solution.py:18
  560.0 6.8 all_gather.11
  566.9 4.0 multiply_convert_fusion
  570.9 6.7 copy.24
  577.6 14.4 %fusion.3 = bf16[2048,1024]{0,1:T(8,128)(2,1)} fusion(bf16[2048,1024]{0,1:T(8,128)(2,1)} %bitcast.91, bf16[2048,2048]{1,0:T(8,128)(2,1)} %all-gather.5.cloned.1.call-done), kind=kOutput, calls=%fused_computation.8 | convolution fusion | flops 8596226048 | bytes 16777216 | tf_op jit(solution)/shard_map/dot_general | solution.py:60
  592.0 6.7 copy.25
  598.7 99.4 %all_to_all.20 = bf16[2048,8,128]{2,1,0:T(8,128)(2,1)S(1)} all-to-all(bf16[2048,8,128]{2,1,0:T(8,128)(2,1)} %copy.25), channel_id=1, replica_groups=mesh['mem'=4,'lon'=8] {'lon'}, dimensions={0} | all-to-all | bytes 8388608 | tf_op jit(solution)/shard_map/all_to_all | solution.py:68
  698.2 6.7 fusion.2
  (25 shorter events, 5.8 us)
Async XLA Ops:
  6.5 27.7 %all-gather.3.cloned.1.call-start = ((), (), s32[]{:S(2)}) async-start(), calls=%async_computation.3 | async-start | bytes 2621440 | tf_op jit(solution)/shard_map/all_gather | solution.py:25
  7.3 154.1 %all-gather.5.cloned.1.call-start = ((), (), s32[]{:S(2)}) async-start(), calls=%async_computation.4 | async-start | bytes 10485760 | tf_op jit(solution)/shard_map/all_gather | solution.py:39
  50.4 99.2 %all-to-all-start = ((bf16[8,256,8,128]{3,2,1,0:T(8,128)(2,1)}), bf16[8,256,8,128]{3,2,1,0:T(8,128)(2,1)}, u32[]{:S(2)}, u32[]{:S(2)}) async-start(bf16[8,256,8,128]{3,2,1,0:T(8,128)(2,1)} %fusion.15), calls=%async_computation | async-start | bytes 8388608 | tf_op jit(solution)/shard_map/all_to_all | solution.py:35
  55.9 7.9 %copy-start = (s32[1,1,32768]{2,1,0:T(1,128)S(1)}, s32[1,1,32768]{2,1,0:T(1,128)}, u32[]{:S(2)}) copy-start(s32[1,1,32768]{2,1,0:T(1,128)} %param.11) | copy-start | bytes 393220
  55.9 151.3 %reduce-scatter.2.cloned.1.call-start = ((), (), s32[]{:S(2)}) async-start(), calls=%async_computation.5 | async-start | bytes 1310720 | tf_op jit(solution)/shard_map/reduce_scatter | solution.py:47
  208.3 180.6 %copy-start.1 = (f32[1,1,32768]{2,1,0:T(1,128)S(1)}, f32[1,1,32768]{2,1,0:T(1,128)}, u32[]{:S(2)}) copy-start(f32[1,1,32768]{2,1,0:T(1,128)} %param.12) | copy-start | bytes 393220
  598.7 99.4 %copy-start.2 = (bf16[256,8,1024]{2,1,0:T(8,128)(2,1)S(1)}, bf16[256,8,1024]{2,1,0:T(8,128)(2,1)}, u32[]{:S(2)}) copy-start(bf16[256,8,1024]{2,1,0:T(8,128)(2,1)} %param.7) | copy-start | bytes 12582916
  598.7 99.4 %copy-start.3 = (bf16[1024,1024]{1,0:T(8,128)(2,1)S(1)}, bf16[1024,1024]{1,0:T(8,128)(2,1)}, u32[]{:S(2)}) copy-start(bf16[1024,1024]{1,0:T(8,128)(2,1)} %all-gather.3.cloned.1.call-done) | copy-start | bytes 6291460
Sparse Core Ops, SparseCore 0:
  8.9 25.2 all-gather.2
  35.8 58.2 all-gather.4
  184.3 22.9 reduce-scatter.1
